TPU v7x, 128 devices: a whole 4x4x4 slice. The times are simulated.
128 devices in a mesh: grp: 2 (over z_hi), pix: 64 (over x, y, z_lo, core).
Axes of the slice: x: 4, y: 4, z: 4 (z_hi: 2, z_lo: 2; z = z_hi * 2 + z_lo), core: 2. Of those that a mesh axis runs over, the one named last changes fastest.
Arguments:
- fields: bfloat16 [2, 2, 128, 512, 512], P('grp', None, None, 'pix'), may hold values from -6 to 6
- lens_phase: float32 [512, 512], P('pix'), may hold values from -3.140625 to 3.140625
- occupancy: float32 [256], replicated, may hold values from 0.05 to 1
- focus_scale: float32 [256], replicated, may hold values from 0.5 to 1.5
- assignment: int32 [256], replicated, may hold values from 0 to 255, each once
- start_basis: float32 [2, 256, 128], replicated, may hold values from -6 to 6
Outputs:
- coherent_modes: bfloat16 [2, 128, 512, 512], P(None, None, 'pix', 'grp')
- relative_power: float32 [128], replicated
Inputs may be any that keep to these rules, and one draw needn't show every extreme that they name: `assignment`: each electron is carried by exactly one wavefront slot.
All inputs are finite; a program needn't handle non-finite values.
Results may differ from a plain program's by a relative error of at most 0.0018.
The roundings to bfloat16 on the way count: a program that leaves them out, or rounds other values in their place, can miss the bound.
Values may be sent and summed in bfloat16 or wider, within the bound.
No kernel may reach another device: no remote copies, remote signals or barrier semaphores. Data moves between devices by JAX's collectives and lax.ppermute only.
A program may use at most 64 MiB of HBM per device.

v0:
```python
import math
import jax
import jax.numpy as jnp
from jax import lax
from jax.sharding import PartitionSpec as P

NROW = 512
NCOL = 512
STEPS = 2


def partner_2(array, axis, apart):
    return lax.ppermute(array, axis, [(i, i ^ 1 << apart) for i in range(lax.axis_size(axis))])


def dft_tables(length):
    index = jnp.arange(length, dtype=jnp.int32)
    product = index[:, None] * index[None, :] % length
    angle = product.astype(jnp.float32) * (2.0 * math.pi / length)
    factor = 1.0 / math.sqrt(length)
    return (
        (jnp.cos(angle) * factor).astype(jnp.bfloat16),
        (jnp.sin(angle) * factor).astype(jnp.bfloat16),
    )


def local(fields, lens_phase, occupancy, focus_scale, assignment, start_basis):
    highest = lax.Precision.HIGHEST
    local_fields = fields[0]
    modes = local_fields.shape[1]
    group_index = lax.axis_index("grp")
    electron = lax.dynamic_slice_in_dim(assignment, group_index * modes, modes)
    choose = (
        electron[:, None] == jnp.arange(assignment.shape[0], dtype=jnp.int32)[None, :]
    ).astype(jnp.float32)
    amplitude = jnp.sqrt(jnp.sum(choose * occupancy[None, :], axis=1))[:, None, None]
    chromatic = jnp.sum(choose * focus_scale[None, :], axis=1)
    angle = chromatic[:, None, None] * lens_phase[None]
    cosine = jnp.cos(angle)
    sine = jnp.sin(angle)
    field_re = local_fields[0].astype(jnp.float32)
    field_im = local_fields[1].astype(jnp.float32)
    phased = jnp.stack(
        [
            amplitude * (field_re * cosine - field_im * sine),
            amplitude * (field_re * sine + field_im * cosine),
        ]
    ).astype(jnp.bfloat16)
    cos_cols, sin_cols = dft_tables(lens_phase.shape[1])
    col_cos = jnp.einsum("zmrc,ck->zmkr", phased, cos_cols, preferred_element_type=jnp.float32)
    col_sin = jnp.einsum("zmrc,ck->zmkr", phased, sin_cols, preferred_element_type=jnp.float32)
    across = jnp.stack([col_cos[0] + col_sin[1], col_cos[1] - col_sin[0]]).astype(jnp.bfloat16)
    full_rows = across.shape[3] * lax.axis_size("pix")
    cos_rows, sin_rows = dft_tables(full_rows)
    pieces = lax.all_to_all(across, "pix", split_axis=2, concat_axis=3, tiled=True)
    row_cos = jnp.dot(pieces, cos_rows, preferred_element_type=jnp.float32)
    row_sin = jnp.dot(pieces, sin_rows, preferred_element_type=jnp.float32)
    focal = jnp.stack([row_cos[0] + row_sin[1], row_cos[1] - row_sin[0]]).astype(jnp.bfloat16)
    stack_size = modes * lax.axis_size("grp")
    half_rows = full_rows // lax.axis_size("grp")
    partner = partner_2(focal, "grp", 0)
    leading = jnp.where(group_index == 0, focal, partner)
    trailing = jnp.where(group_index == 0, partner, focal)
    stacked = jnp.concatenate([leading, trailing], axis=1)
    flat = stacked.reshape(2, stack_size, -1)
    blocks = jnp.einsum("xap,ybp->xyab", flat, flat, preferred_element_type=jnp.float32)
    local_re = blocks[0, 0] + blocks[1, 1]
    local_im = blocks[0, 1] - blocks[1, 0]
    gram_re, gram_im = lax.psum((local_re, local_im), "pix")
    owned = lax.dynamic_slice_in_dim(stacked, group_index * half_rows, half_rows, 3)
    basis_re = start_basis[0]
    basis_im = start_basis[1]
    for iteration in range(STEPS):
        image_re = jnp.dot(gram_re, basis_re, precision=highest) - jnp.dot(
            gram_im, basis_im, precision=highest
        )
        image_im = jnp.dot(gram_re, basis_im, precision=highest) + jnp.dot(
            gram_im, basis_re, precision=highest
        )
        column_norm = jnp.sqrt(jnp.sum(image_re * image_re + image_im * image_im, axis=0) + 1e-06)
        basis_re = image_re / column_norm[None, :]
        basis_im = image_im / column_norm[None, :]
    rounded = jnp.stack([basis_re, basis_im]).astype(jnp.bfloat16)
    rank = rounded.shape[2]
    owned_flat = owned.reshape(2, stack_size, -1)
    products = jnp.einsum("xsk,ysp->xykp", rounded, owned_flat, preferred_element_type=jnp.float32)
    mode_re = products[0, 0] - products[1, 1]
    mode_im = products[0, 1] + products[1, 0]
    energy = lax.psum(jnp.sum(mode_re * mode_re + mode_im * mode_im, axis=1), ("grp", "pix"))
    trace = jnp.sum(jnp.diagonal(gram_re))
    relative_power = energy * stack_size / trace
    inverse = lax.rsqrt(energy / (NROW * NCOL) + 1e-06)
    coherent_modes = (jnp.stack([mode_re, mode_im]) * inverse[None, :, None]).astype(jnp.bfloat16)
    return (coherent_modes.reshape(2, rank, owned.shape[2], owned.shape[3]), relative_power)


def solution(mesh):
    in_specs = (P("grp", None, None, "pix", None), P("pix", None), P(), P(), P(), P())
    out_specs = (P(None, None, "pix", "grp"), P())
    return jax.shard_map(local, mesh=mesh, in_specs=in_specs, out_specs=out_specs, check_vma=False)
```

profile of v0, /device:TPU:1, one launch (start us, length us, event | category | flops | bytes accessed | tf_op | source)
XLA Modules:
  0.0 779.3 jit_solution(8011462047435173882)
XLA Ops:
  7.2 0.0 all-reduce.3.cloned.1.call-start
  7.2 0.8 dynamic_slice.6
  8.0 0.9 select_reduce_fusion.1
  8.9 0.0 copy-start.5
  8.9 1.7 fusion.84
  10.6 0.0 copy-done.5
  10.6 9.2 %fusion.9 = (bf16[1,128,8,512]{3,1,2,0:T(8,128)(2,1)S(1)}, bf16[1,128,8,512]{3,1,2,0:T(8,128)(2,1)S(1)}) fusion(f32[8,512]{1,0:T(8,128)S(1)} %copy-done.5, f32[128]{0:T(128)S(1)} %get-tuple-element.3, f32[128]{0:T(128)S(1)} %sqrt.21, bf16[1,1,128,8,512]{4,3,2,1,0:T(8,128)(2,1)S(1)} %get-tuple-element.18, bf16[1,1,128,8,512]{4,3,2,1,0:T(8,128)(2,1)S(1)} %get-tuple-element.17), kind=kLoop, calls=%fused_computation.18 | loop fusion | flops 6815744 | bytes 4211712 | tf_op jit(solution)/shard_map/convert.10
  19.8 4.9 convolution_bitcast_fusion.2
  24.7 5.0 convolution_bitcast_fusion.1
  29.7 0.5 fusion.17
  30.2 0.2 pad_maximum_fusion.3
  30.4 1.5 copy.51
  31.9 39.1 %all_to_all.18 = bf16[2,128,512,8]{1,3,0,2:T(8,128)(2,1)S(1)} all-to-all(bf16[2,128,512,8]{1,3,0,2:T(8,128)(2,1)S(1)} %copy.51), channel_id=1, replica_groups=mesh['grp'=2,'pix'=64] {'pix'}, dimensions={2} | all-to-all | bytes 4194304 | tf_op jit(solution)/shard_map/all_to_all | solution.py:55
  71.0 4.8 fusion.19
  75.8 4.8 fusion.21
  80.6 1.3 fusion.15
  81.8 1.5 pad_maximum_fusion.4
  83.4 3.6 collective-permute-start
  86.9 46.2 %collective-permute-done = bf16[2,128,8,512]{3,1,2,0:T(8,128)(2,1)} collective-permute-done((bf16[2,128,8,512]{3,1,2,0:T(8,128)(2,1)}, bf16[2,128,8,512]{3,1,2,0:T(8,128)(2,1)}, u32[]{:S(2)}, u32[]{:S(2)}) %collective-permute-start) | collective-permute-done | bytes 2097184 | tf_op jit(solution)/shard_map/ppermute | solution.py:13
  133.2 1.9 broadcast_select_fusion
  135.0 0.0 copy-start.1
  135.0 0.0 copy-start.2
  135.0 2.4 fusion.25
  137.4 0.0 copy-done.1
  137.4 0.0 copy-done.2
  137.4 0.9 fusion.42
  138.3 0.0 all-reduce.3.cloned.1.call-update
  138.4 3.1 fusion.13
  141.5 0.0 copy-start.4
  141.5 2.9 copy.56
  144.4 544.8 %all-reduce.3.cloned.1.call-done = (f32[256,256]{0,1:T(8,128)}, f32[256,256]{0,1:T(8,128)}) async-done(((f32[256,256]{0,1:T(8,128)}, f32[256,256]{0,1:T(8,128)}), (f32[256,256]{0,1:T(8,128)}, f32[256,256]{0,1:T(8,128)})) %all-reduce.3.cloned.1.call-update) | async-done | bytes 524304 | tf_op jit(solution)/shard_map/psum | solution.py:69
  689.1 0.0 copy-start
  689.1 0.0 copy-start.3
  689.1 0.0 copy-done.4
  689.2 1.6 fusion.50
  690.8 1.5 fusion.46
  692.3 1.5 convolution_subtract_fusion.1
  693.9 1.6 add_reduce_fusion.2
  695.4 0.0 copy-done
  695.4 0.6 fusion.58
  696.0 0.6 fusion.59
  696.6 0.0 copy-done.3
  696.6 0.6 convolution_subtract_fusion
  697.2 0.6 add_reduce_fusion.1
  697.9 0.7 convolution_bitcast_fusion
  698.6 0.3 add_reduce_fusion
  698.9 67.0 %psum.23 = f32[128]{0:T(128)S(1)} all-reduce(f32[128]{0:T(128)S(1)} %get-tuple-element.6), channel_id=1, replica_groups=mesh['grp'=2,'pix'=64] {'grp','pix'}, use_global_device_ids=true, to_apply=%region_7.8 | all-reduce | flops 128 | bytes 1024 | tf_op jit(solution)/shard_map/psum | solution.py:89
  766.0 2.4 gather_fusion
  768.3 0.5 copy.57
  768.8 0.5 copy.58
  769.3 0.6 reduce_sum.59
  769.9 1.2 multiply_divide_fusion
  771.1 1.2 fusion.18
  (5 shorter events, 0.1 us)
Async XLA Ops:
  7.2 682.0 %all-reduce.3.cloned.1.call-start = ((), (), s32[]{:S(2)}) async-start(), calls=%async_computation.1 | async-start | bytes 1048576 | tf_op jit(solution)/shard_map/psum | solution.py:69
  8.9 1.7 copy-start.5
  83.4 49.8 %collective-permute-start = (bf16[2,128,8,512]{3,1,2,0:T(8,128)(2,1)}, bf16[2,128,8,512]{3,1,2,0:T(8,128)(2,1)}, u32[]{:S(2)}, u32[]{:S(2)}) collective-permute-start(bf16[2,128,8,512]{3,1,2,0:T(8,128)(2,1)} %pad_maximum_fusion.4), channel_id=1, source_target_pairs={{0,64},{64,0},{1,65},{65,1},{2,66},{66,2},{3,67},{67,3},{4,68},{68... | collective-permute-start | bytes 6291464 | tf_op jit(solution)/shard_map/ppermute | solution.py:13
  135.0 2.4 copy-start.1
  135.0 2.4 copy-start.2
  141.5 547.7 %copy-start.4 = (f32[2,256,128]{2,1,0:T(8,128)S(1)}, f32[2,256,128]{2,1,0:T(8,128)}, u32[]{:S(2)}) copy-start(f32[2,256,128]{2,1,0:T(8,128)} %param.11) | copy-start | bytes 786436
  689.1 6.3 copy-start
  689.1 7.5 copy-start.3
Sparse Core Ops, SparseCore 0:
  138.5 550.6 all-reduce.2
where the time goes:
time: 782 us; the launch traced here: 779 us
  waiting for transfers between devices  591 us (76%)
  blocking collectives  106 us (14%)
  matrix products  31.2 us (4%)
  other arithmetic  22.7 us (3%)
  between operations  14.5 us (2%)
  local copies, waits for them, and re-layouts  10.2 us (1%)
    psum x1, waiting for transfers between devices, local(): gram_re, gram_im = lax.psum((local_re, local_im), 'pix')  545 us
    psum x1, blocking collectives, local(): lax.psum(jnp.sum(mode_re * mode_re + mode_im * mode_im, axis=1), ('grp',...  67 us
    ppermute x1, waiting for transfers between devices, partner_2(): lax.ppermute(array, axis, [(i, i ^ 1 << apart) for i in range(lax.axis_si...  46.2 us
    all_to_all x1, blocking collectives, local(): lax.all_to_all(across, 'pix', split_axis=2, concat_axis=3, tiled=True)  39.1 us
  transfers between devices with their start and end apart: 2, of which 2 were waited for; matrix products, arithmetic and copies ran while one was open for 1% of the time, Pallas kernels for 0%

commit v1 on v0

--- a/solution.py
+++ b/solution.py
@@ -86,7 +86,10 @@
     products = jnp.einsum("xsk,ysp->xykp", rounded, owned_flat, preferred_element_type=jnp.float32)
     mode_re = products[0, 0] - products[1, 1]
     mode_im = products[0, 1] + products[1, 0]
-    energy = lax.psum(jnp.sum(mode_re * mode_re + mode_im * mode_im, axis=1), ("grp", "pix"))
+    energy = jnp.sum(
+        lax.all_gather(jnp.sum(mode_re * mode_re + mode_im * mode_im, axis=1), ("grp", "pix")),
+        axis=0,
+    )
     trace = jnp.sum(jnp.diagonal(gram_re))
     relative_power = energy * stack_size / trace
     inverse = lax.rsqrt(energy / (NROW * NCOL) + 1e-06)

time: 782 us -> 893 us (1.14)
  blocking collectives: 106 us -> 216 us
    all_gather x0 -> x1, blocking collectives: none -> 177 us  [local(): lax.all_gather(jnp.sum(mode_re * mode_re + mode_im * mode_im, axis=1), ('...]
    psum x1 -> x0, blocking collectives: 67 us -> none  [local(): lax.psum(jnp.sum(mode_re * mode_re + mode_im * mode_im, axis=1), ('grp',...]
where the time goes in v1:
time: 893 us; the launch traced here: 890 us
  waiting for transfers between devices  591 us (66%)
  blocking collectives  216 us (24%)
  matrix products  31.2 us (3%)
  other arithmetic  22.8 us (3%)
  between operations  14.5 us (2%)
  local copies, waits for them, and re-layouts  10.2 us (1%)
    psum x1, waiting for transfers between devices, local(): gram_re, gram_im = lax.psum((local_re, local_im), 'pix')  545 us
    all_gather x1, blocking collectives, local(): lax.all_gather(jnp.sum(mode_re * mode_re + mode_im * mode_im, axis=1), ('...  177 us
    ppermute x1, waiting for transfers between devices, partner_2(): lax.ppermute(array, axis, [(i, i ^ 1 << apart) for i in range(lax.axis_si...  46.2 us
    all_to_all x1, blocking collectives, local(): lax.all_to_all(across, 'pix', split_axis=2, concat_axis=3, tiled=True)  39.1 us
  transfers between devices with their start and end apart: 2, of which 2 were waited for; matrix products, arithmetic and copies ran while one was open for 1% of the time, Pallas kernels for 0%

profile of v1, /device:TPU:1, one launch (start us, length us, event | category | flops | bytes accessed | tf_op | source)
XLA Modules:
  0.0 889.7 jit_solution(17494671391567531645)
XLA Ops:
  7.2 0.0 all-reduce.3.cloned.1.call-start
  7.2 0.8 dynamic_slice.6
  8.0 0.9 select_reduce_fusion.1
  8.9 0.0 copy-start.5
  8.9 1.7 fusion.84
  10.6 0.0 copy-done.5
  10.6 9.2 %fusion.9 = (bf16[1,128,8,512]{3,1,2,0:T(8,128)(2,1)S(1)}, bf16[1,128,8,512]{3,1,2,0:T(8,128)(2,1)S(1)}) fusion(f32[8,512]{1,0:T(8,128)S(1)} %copy-done.5, f32[128]{0:T(128)S(1)} %get-tuple-element.3, f32[128]{0:T(128)S(1)} %sqrt.21, bf16[1,1,128,8,512]{4,3,2,1,0:T(8,128)(2,1)S(1)} %get-tuple-element.18, bf16[1,1,128,8,512]{4,3,2,1,0:T(8,128)(2,1)S(1)} %get-tuple-element.17), kind=kLoop, calls=%fused_computation.18 | loop fusion | flops 6815744 | bytes 4211712 | tf_op jit(solution)/shard_map/convert.10
  19.8 4.9 convolution_bitcast_fusion.2
  24.7 5.0 convolution_bitcast_fusion.1
  29.7 0.5 fusion.17
  30.2 0.2 pad_maximum_fusion.3
  30.4 1.5 copy.51
  31.9 39.1 %all_to_all.18 = bf16[2,128,512,8]{1,3,0,2:T(8,128)(2,1)S(1)} all-to-all(bf16[2,128,512,8]{1,3,0,2:T(8,128)(2,1)S(1)} %copy.51), channel_id=1, replica_groups=mesh['grp'=2,'pix'=64] {'pix'}, dimensions={2} | all-to-all | bytes 4194304 | tf_op jit(solution)/shard_map/all_to_all | solution.py:55
  71.0 4.8 fusion.19
  75.8 4.8 fusion.21
  80.6 1.3 fusion.15
  81.8 1.5 pad_maximum_fusion.4
  83.4 3.6 collective-permute-start
  86.9 46.2 %collective-permute-done = bf16[2,128,8,512]{3,1,2,0:T(8,128)(2,1)} collective-permute-done((bf16[2,128,8,512]{3,1,2,0:T(8,128)(2,1)}, bf16[2,128,8,512]{3,1,2,0:T(8,128)(2,1)}, u32[]{:S(2)}, u32[]{:S(2)}) %collective-permute-start) | collective-permute-done | bytes 2097184 | tf_op jit(solution)/shard_map/ppermute | solution.py:13
  133.2 1.9 broadcast_select_fusion
  135.0 0.0 copy-start.1
  135.0 0.0 copy-start.2
  135.0 2.4 fusion.25
  137.4 0.0 copy-done.1
  137.4 0.0 copy-done.2
  137.4 0.9 fusion.42
  138.3 0.0 all-reduce.3.cloned.1.call-update
  138.4 3.1 fusion.13
  141.5 0.0 copy-start.4
  141.5 2.9 copy.56
  144.4 544.8 %all-reduce.3.cloned.1.call-done = (f32[256,256]{0,1:T(8,128)}, f32[256,256]{0,1:T(8,128)}) async-done(((f32[256,256]{0,1:T(8,128)}, f32[256,256]{0,1:T(8,128)}), (f32[256,256]{0,1:T(8,128)}, f32[256,256]{0,1:T(8,128)})) %all-reduce.3.cloned.1.call-update) | async-done | bytes 524304 | tf_op jit(solution)/shard_map/psum | solution.py:69
  689.1 0.0 copy-start
  689.1 0.0 copy-start.3
  689.1 0.0 copy-done.4
  689.2 1.6 fusion.50
  690.8 1.5 fusion.46
  692.3 1.5 convolution_subtract_fusion.1
  693.9 1.6 add_reduce_fusion.2
  695.4 0.0 copy-done
  695.4 0.6 fusion.58
  696.0 0.6 fusion.59
  696.6 0.0 copy-done.3
  696.6 0.6 convolution_subtract_fusion
  697.2 0.6 add_reduce_fusion.1
  697.9 0.7 convolution_bitcast_fusion
  698.6 0.3 add_reduce_fusion
  698.9 177.2 %all-gather.1 = f32[128,1,128]{2,1,0:T(1,128)S(1)} all-gather(f32[1,1,128]{2,1,0:T(1,128)S(1)} %bitcast.105), channel_id=2, replica_groups=mesh['grp'=2,'pix'=64] {'grp','pix'}, dimensions={0}, use_global_device_ids=true | all-gather | bytes 66048 | tf_op jit(solution)/shard_map/all_gather | solution.py:90
  876.2 2.4 gather_fusion
  878.6 0.2 reduce_sum.68
  878.7 0.6 reduce_sum.69
  879.3 0.5 copy.57
  879.8 0.5 copy.58
  880.3 1.2 multiply_divide_fusion
  881.4 1.2 fusion.18
  (5 shorter events, 0.1 us)
Async XLA Ops:
  7.2 682.0 %all-reduce.3.cloned.1.call-start = ((), (), s32[]{:S(2)}) async-start(), calls=%async_computation.1 | async-start | bytes 1048576 | tf_op jit(solution)/shard_map/psum | solution.py:69
  8.9 1.7 copy-start.5
  83.4 49.8 %collective-permute-start = (bf16[2,128,8,512]{3,1,2,0:T(8,128)(2,1)}, bf16[2,128,8,512]{3,1,2,0:T(8,128)(2,1)}, u32[]{:S(2)}, u32[]{:S(2)}) collective-permute-start(bf16[2,128,8,512]{3,1,2,0:T(8,128)(2,1)} %pad_maximum_fusion.4), channel_id=1, source_target_pairs={{0,64},{64,0},{1,65},{65,1},{2,66},{66,2},{3,67},{67,3},{4,68},{68... | collective-permute-start | bytes 6291464 | tf_op jit(solution)/shard_map/ppermute | solution.py:13
  135.0 2.4 copy-start.1
  135.0 2.4 copy-start.2
  141.5 547.7 %copy-start.4 = (f32[2,256,128]{2,1,0:T(8,128)S(1)}, f32[2,256,128]{2,1,0:T(8,128)}, u32[]{:S(2)}) copy-start(f32[2,256,128]{2,1,0:T(8,128)} %param.11) | copy-start | bytes 786436
  689.1 6.3 copy-start
  689.1 7.5 copy-start.3
Sparse Core Ops, SparseCore 0:
  138.5 550.6 all-reduce.2
